TPU v7x, 256 devices: a whole 4x4x8 slice. The times are simulated.
256 devices in a mesh: context: 16 (over z, core), heads: 16 (over x, y).
Axes of the slice: x: 4, y: 4, z: 8, core: 2. Of those that a mesh axis runs over, the one named last changes fastest.
Arguments:
- main_query: bfloat16 [256, 128, 576], P('context', 'heads'), may hold values from -6 to 6
- latent_keys: bfloat16 [32768, 576], P('context'), may hold values from -6 to 6
- head_lse: float32 [256, 128], P(None, 'heads'), may hold values from 4 to 8
- lengths: int32 [256], replicated, may hold values from 1 to 32768, as said below
- index_query: bfloat16 [256, 64, 128], P('heads'), may hold values from -256 to 256
- index_key: bfloat16 [32768, 128], P('context'), may hold values from -8 to 8
- index_weight: float32 [256, 64], P('heads'), may hold values from -2.4 to 2.4
Outputs:
- grad_index_query: float32 [256, 64, 128], P('heads', 'context')
- grad_index_key: float32 [32768, 128], P(('context', 'heads'))
Inputs may be any that keep to these rules, and one draw needn't show every extreme that they name: Query rows come in blocks of 16 consecutive rows whose lengths rise by one from row to row; some block ends at the last key.
All inputs are finite; a program needn't handle non-finite values.
Results may differ from a plain program's by a relative error of at most 0.0029.
Values may be sent and summed in bfloat16 or wider, within the bound.
A program may use at most 64 MiB of HBM per device.

v0:
```python
import math
import jax
import jax.numpy as jnp
from jax import lax
from jax.sharding import PartitionSpec as P

main_scale = 192.0 ** (-0.5)
loss_scale = 64.0
masked_low = -1e30


def head_mass(queries, lse_rows, len_rows, latent, first_key):
    row_count = queries.shape[0]
    block_rows = math.gcd(row_count, 64)
    steps_count = row_count // block_rows
    key_pos = first_key + jnp.arange(latent.shape[0], dtype=jnp.int32)

    def one_block(inputs):
        query_block, lse_block, len_block = inputs
        scores = (
            jnp.einsum("rhd,sd->rhs", query_block, latent, preferred_element_type=jnp.float32)
            * main_scale
        )
        summed = jnp.sum(jnp.exp(scores - lse_block[:, :, None]), axis=1)
        return jnp.where(key_pos[None, :] < len_block[:, None], summed, 0.0)

    stacked = lax.map(
        one_block,
        (
            queries.reshape((steps_count, block_rows) + queries.shape[1:]),
            lse_rows.reshape(steps_count, block_rows, lse_rows.shape[1]),
            len_rows.reshape(steps_count, block_rows),
        ),
    )
    return stacked.reshape(row_count, latent.shape[0])


def on_device(main_query, latent_keys, head_lse, lengths, index_query, index_key, index_weight):
    key_count = latent_keys.shape[0]
    first_key = lax.axis_index("context") * key_count
    own_rows = index_query.shape[0]
    row_first = lax.axis_index("heads") * own_rows
    partial_mass = head_mass(
        lax.all_gather(main_query, "context", axis=0, tiled=True),
        head_lse,
        lengths,
        latent_keys,
        first_key,
    )
    summed_mass = lax.psum(partial_mass, "heads")
    row_mass = lax.dynamic_slice_in_dim(summed_mass, row_first, own_rows, 0)
    own_len = lax.dynamic_slice_in_dim(lengths, row_first, own_rows, 0)
    visible = (first_key + jnp.arange(key_count, dtype=jnp.int32))[None, :] < own_len[:, None]
    heads_count = index_query.shape[1]
    width = index_query.shape[2]
    index_scale = width ** (-0.5)
    flat_query = index_query.reshape(own_rows * heads_count, width)
    block_keys = math.gcd(key_count, 512)
    block_total = key_count // block_keys
    key_blocks = index_key.reshape(block_total, block_keys, width)

    def block_dots(key_block):
        products = lax.dot_general(
            flat_query, key_block, (((1,), (1,)), ((), ())), preferred_element_type=jnp.float32
        )
        return products.reshape(own_rows, heads_count, key_block.shape[0])

    def block_logits(key_block):
        return (
            jnp.einsum(
                "tj,tjs->ts",
                index_weight,
                jax.nn.relu(block_dots(key_block)),
                precision=lax.Precision.HIGHEST,
            )
            * index_scale
        )

    logits = jnp.moveaxis(lax.map(block_logits, key_blocks), 0, 1).reshape(own_rows, key_count)
    local_top = jnp.max(jnp.where(visible, logits, masked_low), axis=1)
    mass_local = jnp.sum(row_mass, axis=1)
    top = lax.pmax(local_top, "context")
    weights_exp = jnp.where(visible, jnp.exp(logits - top[:, None]), 0.0)
    share_sum, mass_total = lax.psum((jnp.sum(weights_exp, axis=1), mass_local), "context")
    probability = weights_exp / share_sum[:, None]
    target = row_mass / mass_total[:, None]
    slopes = loss_scale * (probability - target)
    slope_blocks = slopes.reshape(own_rows, block_total, block_keys).transpose(1, 0, 2)

    def back_step(query_grad, inputs):
        key_block, slope_block = inputs
        products = block_dots(key_block)
        terms = jnp.where(
            products > 0, slope_block[:, None, :] * index_weight[:, :, None] * index_scale, 0.0
        )
        terms = terms.astype(jnp.bfloat16).reshape(own_rows * heads_count, key_block.shape[0])
        query_grad = query_grad + jnp.dot(terms, key_block, preferred_element_type=jnp.float32)
        key_grad = lax.dot_general(
            terms, flat_query, (((0,), (0,)), ((), ())), preferred_element_type=jnp.float32
        )
        return (query_grad, key_grad)

    start_grad = jnp.zeros((own_rows * heads_count, width), jnp.float32)
    query_grad, key_grads = lax.scan(back_step, start_grad, (key_blocks, slope_blocks))
    query_grad = query_grad.reshape(own_rows, heads_count, width)
    key_grad = key_grads.reshape(key_count, width)
    out_query = lax.psum_scatter(query_grad, "context", scatter_dimension=1, tiled=True)
    out_key = lax.psum_scatter(key_grad, "heads", scatter_dimension=0, tiled=True)
    return (out_query, out_key)


def solution(mesh):
    placed = (
        P("context", "heads", None),
        P("context", None),
        P(None, "heads"),
        P(),
        P("heads", None, None),
        P("context", None),
        P("heads", None),
    )
    return jax.shard_map(
        on_device,
        mesh=mesh,
        in_specs=placed,
        out_specs=(P("heads", "context", None), P(("context", "heads"), None)),
        check_vma=False,
    )
```

profile of v0, /device:TPU:2, one launch (start us, length us, event | category | flops | bytes accessed | tf_op | source)
XLA Modules:
  0.0 374.9 jit_solution(15053279912884742428)
XLA Ops:
  11.1 41.8 %all-gather.2.cloned.1.call-done = bf16[256,8,576]{2,1,0:T(8,128)(2,1)} async-done(((bf16[16,8,576]{2,1,0:T(8,128)(2,1)}), bf16[256,8,576]{2,1,0:T(8,128)(2,1)}) %all-gather.2.cloned.1.call-update) | async-done | bytes 2359312 | tf_op jit(solution)/shard_map/all_gather | solution.py:44
  52.9 22.9 %while.36 = (s32[]{:T(128)}, f32[4,64,2048]{2,1,0:T(8,128)}, s32[4,64]{1,0:T(4,128)S(1)}, bf16[4,64,8,576]{3,2,1,0:T(8,128)(2,1)}, bf16[2048,576]{0,1:T(8,128)(2...) while((s32[]{:T(128)}, f32[4,64,2048]{2,1,0:T(8,128)}, s32[4,64]{1,0:T(4,128)S(1)}, ...), condition=%wide.region_8.9_spmd.clone, body=%wide.region_6.8_spmd.clone.sunk | while | flops 1211238400 | bytes 4611937 | solution.py:27
  52.9 4.8 %exponential_reduce_fusion.2 = f32[64,2048]{1,0:T(8,128)S(1)} fusion(bf16[2048,576]{0,1:T(8,128)(2,1)} %get-tuple-element.382, f32[64,8]{1,0:T(8,128)S(1)} %dynamic-slice_bitcast_fusion.5, bf16[4,64,8,576]{3,2,1,0:T(8,128)(2,1)} %get-tuple-element.381, s32[]{:T(128)} %get-tuple-element.370), kind=kOutput, calls=%fused_computation.7.clone.1 | convolution fusion | flops 1210974208 | bytes 3541504 | tf_op jit(solution)/shard_map/while/body/eval_jaxpr/rhd,sd->rhs/dot_general | solution.py:21
  58.6 4.8 %exponential_reduce_fusion.2 = f32[64,2048]{1,0:T(8,128)S(1)} fusion(bf16[2048,576]{0,1:T(8,128)(2,1)} %get-tuple-element.382, f32[64,8]{1,0:T(8,128)S(1)} %dynamic-slice_bitcast_fusion.5, bf16[4,64,8,576]{3,2,1,0:T(8,128)(2,1)} %get-tuple-element.381, s32[]{:T(128)} %get-tuple-element.370), kind=kOutput, calls=%fused_computation.7.clone.1 | convolution fusion | flops 1210974208 | bytes 3541504 | tf_op jit(solution)/shard_map/while/body/eval_jaxpr/rhd,sd->rhs/dot_general | solution.py:21
  64.3 4.8 %exponential_reduce_fusion.2 = f32[64,2048]{1,0:T(8,128)S(1)} fusion(bf16[2048,576]{0,1:T(8,128)(2,1)} %get-tuple-element.382, f32[64,8]{1,0:T(8,128)S(1)} %dynamic-slice_bitcast_fusion.5, bf16[4,64,8,576]{3,2,1,0:T(8,128)(2,1)} %get-tuple-element.381, s32[]{:T(128)} %get-tuple-element.370), kind=kOutput, calls=%fused_computation.7.clone.1 | convolution fusion | flops 1210974208 | bytes 3541504 | tf_op jit(solution)/shard_map/while/body/eval_jaxpr/rhd,sd->rhs/dot_general | solution.py:21
  70.0 4.8 %exponential_reduce_fusion.2 = f32[64,2048]{1,0:T(8,128)S(1)} fusion(bf16[2048,576]{0,1:T(8,128)(2,1)} %get-tuple-element.382, f32[64,8]{1,0:T(8,128)S(1)} %dynamic-slice_bitcast_fusion.5, bf16[4,64,8,576]{3,2,1,0:T(8,128)(2,1)} %get-tuple-element.381, s32[]{:T(128)} %get-tuple-element.370), kind=kOutput, calls=%fused_computation.7.clone.1 | convolution fusion | flops 1210974208 | bytes 3541504 | tf_op jit(solution)/shard_map/while/body/eval_jaxpr/rhd,sd->rhs/dot_general | solution.py:21
  76.9 19.8 %while.35 = (s32[]{:T(128)}, f32[4,16,512]{2,1,0:T(8,128)S(1)}, bf16[4,512,128]{2,1,0:T(8,128)(2,1)S(1)}, bf16[1024,128]{1,0:T(8,128)(2,1)S(1)}, f32[16,64]{1,0:T(8,128)S(1)}, /*index=5*/s32[]{:T(128)}) while((s32[]{:T(128)}, f32[4,16,512]{2,1,0:T(8,128)S(1)}, bf16[4,512,128]{2,1,0:T(8,128)(2,1)S(1)}, bf16[1024,128]{1,0:T(8,128)(2,1)S(1)}, ...), condition=%wide.region_1.2_spmd, body=%wide.region_0.1_spmd.sunk | while | flops 141041664 | bytes 8884301 | solution.py:79
  76.9 1.8 maximum_bitcast_fusion.2
  78.7 1.9 copy.41
  81.8 1.8 maximum_bitcast_fusion.2
  83.6 1.9 copy.41
  85.6 1.2 fusion.56
  86.8 1.8 maximum_bitcast_fusion.2
  88.6 1.9 copy.41
  90.5 1.2 fusion.56
  91.8 1.8 maximum_bitcast_fusion.2
  93.6 1.9 copy.41
  97.0 24.9 %pmax.7 = f32[16]{0:T(128)S(1)} all-reduce(f32[16]{0:T(128)S(1)} %fusion.18), channel_id=1, replica_groups=mesh['context'=16,'heads'=16] {'context'}, use_global_device_ids=true, to_apply=%region_3.4 | all-reduce | flops 16 | bytes 128 | tf_op jit(solution)/shard_map/pmax | solution.py:82
  122.1 53.3 %all-reduce.3.cloned.1.call-done = f32[256,2048]{1,0:T(8,128)} async-done(((f32[256,2048]{1,0:T(8,128)}), f32[256,2048]{1,0:T(8,128)}) %all-reduce.3.cloned.1.call-update) | async-done | bytes 2097168 | tf_op jit(solution)/shard_map/psum | solution.py:50
  176.4 24.2 %all-reduce = (f32[16]{0:T(128)S(1)}, f32[16]{0:T(128)S(1)}) all-reduce(f32[16]{0:T(128)S(1)} %dynamic-slice_reduce_fusion, f32[16]{0:T(128)S(1)} %fusion.19), channel_id=1, replica_groups=mesh['context'=16,'heads'=16] {'context'}, use_global_device_ids=true, to_apply=%region_11.12 | all-reduce | flops 32 | bytes 256 | tf_op jit(solution)/shard_map/psum | solution.py:84
  202.3 26.9 %while.37 = (s32[]{:T(128)}, f32[1024,128]{1,0:T(8,128)S(1)}, f32[4,512,128]{2,1,0:T(8,128)}, bf16[4,512,128]{2,1,0:T(8,128)(2,1)S(1)}, bf16[1024,128]{1,0:T(8,1...) while((s32[]{:T(128)}, f32[1024,128]{1,0:T(8,128)S(1)}, ...), condition=%wide.wide.region_13.14_spmd.clone, body=%wide.wide.region_12.13_spmd.clone.sunk | while | flops 405536768 | bytes 13734523 | solution.py:104
  203.3 1.8 copy.42
  205.2 2.1 select_convert_fusion.3
  210.0 1.8 copy.42
  211.9 2.1 select_convert_fusion.3
  216.8 1.8 copy.42
  218.6 2.1 select_convert_fusion.3
  223.5 1.8 copy.42
  225.3 2.1 select_convert_fusion.3
  231.0 56.1 %reduce-scatter.3.cloned.1.call-done = f32[16,4,128]{2,0,1:T(8,128)} async-done(((f32[16,64,128]{2,0,1:T(8,128)}), f32[16,4,128]{2,0,1:T(8,128)}) %reduce-scatter.3.cloned.1.call-update) | async-done | bytes 32784 | tf_op jit(solution)/shard_map/reduce_scatter | solution.py:107
  287.1 1.4 copy.28
  288.5 79.9 %reduce-scatter.5.cloned.1.call-done = f32[128,128]{1,0:T(8,128)} async-done(((f32[2048,128]{1,0:T(8,128)}), f32[128,128]{1,0:T(8,128)}) %reduce-scatter.5.cloned.1.call-update) | async-done | bytes 65552 | tf_op jit(solution)/shard_map/reduce_scatter | solution.py:108
  (69 shorter events, 27.2 us)
Async XLA Ops:
  7.2 45.7 %all-gather.2.cloned.1.call-start = ((), (), s32[]{:S(2)}) async-start(), calls=%async_computation.2 | async-start | bytes 2785280 | tf_op jit(solution)/shard_map/all_gather | solution.py:44
  7.9 167.5 %all-reduce.3.cloned.1.call-start = ((), (), s32[]{:S(2)}) async-start(), calls=%async_computation.3 | async-start | bytes 4194304 | tf_op jit(solution)/shard_map/psum | solution.py:50
  75.8 0.9 copy-start
  75.8 1.1 copy-start.1
  75.8 1.1 copy-start.2
  75.8 211.3 %reduce-scatter.3.cloned.1.call-start = ((), (), s32[]{:S(2)}) async-start(), calls=%async_computation.4 | async-start | bytes 557056 | tf_op jit(solution)/shard_map/reduce_scatter | solution.py:107
  230.4 138.0 %reduce-scatter.5.cloned.1.call-start = ((), (), s32[]{:S(2)}) async-start(), calls=%async_computation.5 | async-start | bytes 1114112 | tf_op jit(solution)/shard_map/reduce_scatter | solution.py:108
Sparse Core Ops, SparseCore 0:
  9.8 43.0 all-gather.1
  75.9 99.3 all-reduce.2
  230.5 56.5 reduce-scatter.2
  291.0 77.3 reduce-scatter.4
where the time goes:
time: 376 us; the launch traced here: 375 us
  waiting for transfers between devices  232 us (62%)
  blocking collectives  49.1 us (13%)
  matrix products  46.5 us (12%)
  local copies, waits for them, and re-layouts  26.4 us (7%)
  between operations  13.8 us (4%)
  other arithmetic  6.2 us (2%)
    reduce_scatter x1, waiting for transfers between devices, on_device(): lax.psum_scatter(key_grad, 'heads', scatter_dimension=0, tiled=True)  79.9 us
    reduce_scatter x1, waiting for transfers between devices, on_device(): lax.psum_scatter(query_grad, 'context', scatter_dimension=1, tiled=True)  56.1 us
    psum x1, waiting for transfers between devices, on_device(): summed_mass = lax.psum(partial_mass, 'heads')  53.3 us
    all_gather x1, waiting for transfers between devices, on_device(): lax.all_gather(main_query, 'context', axis=0, tiled=True)  41.8 us
    pmax x1, blocking collectives, on_device(): top = lax.pmax(local_top, 'context')  24.9 us
    psum x1, blocking collectives, on_device(): lax.psum((jnp.sum(weights_exp, axis=1), mass_local), 'context')  24.2 us
    dot_general x4, matrix products, one_block(): jnp.einsum('rhd,sd->rhs', query_block, latent, preferred_element_type=jnp...  19 us
    dot_general x8, matrix products, block_dots(): lax.dot_general(flat_query, key_block, (((1,), (1,)), ((), ())), preferre...  15.5 us
  transfers between devices with their start and end apart: 4, of which 4 were waited for; matrix products, arithmetic and copies ran while one was open for 7% of the time, Pallas kernels for 0%

commit v1 on v0

--- a/solution.py
+++ b/solution.py
@@ -40,12 +40,12 @@
     first_key = lax.axis_index("context") * key_count
     own_rows = index_query.shape[0]
     row_first = lax.axis_index("heads") * own_rows
+    settle_views = lambda u_in, group_axis: jnp.concatenate(
+        jax.lax.all_to_all(jnp.stack([u_in] * jax.lax.axis_size(group_axis)), group_axis, 0, 0),
+        axis=0,
+    )
     partial_mass = head_mass(
-        lax.all_gather(main_query, "context", axis=0, tiled=True),
-        head_lse,
-        lengths,
-        latent_keys,
-        first_key,
+        settle_views(main_query, group_axis="context"), head_lse, lengths, latent_keys, first_key
     )
     summed_mass = lax.psum(partial_mass, "heads")
     row_mass = lax.dynamic_slice_in_dim(summed_mass, row_first, own_rows, 0)

time: 376 us -> 400 us (1.064)
  waiting for transfers between devices: 232 us -> 251 us
  starting transfers between devices: 0.16 us -> 8.88 us
    all_to_all x0 -> x1, waiting for transfers between devices: none -> 60.1 us  [on_device(): jax.lax.all_to_all(jnp.stack([u_in] * jax.lax.axis_size(group_axis)), gro...]
    all_gather x1 -> x0, waiting for transfers between devices: 41.8 us -> none  [on_device(): lax.all_gather(main_query, 'context', axis=0, tiled=True)]
    all_to_all x0 -> x1, starting transfers between devices: none -> 8.76 us  [on_device(): jax.lax.all_to_all(jnp.stack([u_in] * jax.lax.axis_size(group_axis)), gro...]
  transfers between devices with their start and end apart: 4 -> 4, of which waited for: 4 -> 4; matrix products, arithmetic and copies ran while one was open for 7% -> 5% of each run, Pallas kernels for 0% -> 0%
where the time goes in v1:
time: 400 us; the launch traced here: 399 us
  waiting for transfers between devices  251 us (63%)
  blocking collectives  48.6 us (12%)
  matrix products  43.1 us (11%)
  local copies, waits for them, and re-layouts  26.6 us (7%)
  between operations  13.9 us (3%)
  starting transfers between devices  8.88 us (2%)
  other arithmetic  6.21 us (2%)
    reduce_scatter x1, waiting for transfers between devices, on_device(): lax.psum_scatter(key_grad, 'heads', scatter_dimension=0, tiled=True)  80 us
    all_to_all x1, waiting for transfers between devices, on_device(): jax.lax.all_to_all(jnp.stack([u_in] * jax.lax.axis_size(group_axis)), gro...  60.1 us
    reduce_scatter x1, waiting for transfers between devices, on_device(): lax.psum_scatter(query_grad, 'context', scatter_dimension=1, tiled=True)  56 us
    psum x1, waiting for transfers between devices, on_device(): summed_mass = lax.psum(partial_mass, 'heads')  54.5 us
    pmax x1, blocking collectives, on_device(): top = lax.pmax(local_top, 'context')  24.4 us
    psum x1, blocking collectives, on_device(): lax.psum((jnp.sum(weights_exp, axis=1), mass_local), 'context')  24.2 us
    dot_general x4, matrix products, one_block(): jnp.einsum('rhd,sd->rhs', query_block, latent, preferred_element_type=jnp...  15.9 us
    dot_general x8, matrix products, block_dots(): lax.dot_general(flat_query, key_block, (((1,), (1,)), ((), ())), preferre...  15.3 us
  transfers between devices with their start and end apart: 4, of which 4 were waited for; matrix products, arithmetic and copies ran while one was open for 5% of the time, Pallas kernels for 0%

profile of v1, /device:TPU:2, one launch (start us, length us, event | category | flops | bytes accessed | tf_op | source)
XLA Modules:
  0.0 398.8 jit_solution(3548400001475974303)
XLA Ops:
  7.2 2.8 stack.2
  9.9 8.8 %all-to-all-start = ((bf16[16,16,8,576]{3,2,1,0:T(8,128)(2,1)}), bf16[16,16,8,576]{3,2,1,0:T(8,128)(2,1)}, u32[]{:S(2)}, u32[]{:S(2)}) async-start(bf16[16,16,8,576]{3,2,1,0:T(8,128)(2,1)} %stack.2), calls=%async_computation | async-start | bytes 5242880 | tf_op jit(solution)/shard_map/all_to_all | solution.py:44
  19.2 60.1 %all-to-all-done = bf16[16,16,8,576]{3,2,1,0:T(8,128)(2,1)} async-done(((bf16[16,16,8,576]{3,2,1,0:T(8,128)(2,1)}), bf16[16,16,8,576]{3,2,1,0:T(8,128)(2,1)}, u32[]{:S(2)}, u32[]{:S(2)}) %all-to-all-start) | async-done | bytes 2359328 | tf_op jit(solution)/shard_map/all_to_all | solution.py:44
  79.3 19.8 %while.36 = (s32[]{:T(128)}, f32[4,64,2048]{2,1,0:T(8,128)}, s32[4,64]{1,0:T(4,128)S(1)}, bf16[4,64,8,576]{3,2,1,0:T(8,128)(2,1)}, bf16[2048,576]{0,1:T(8,128)(2...) while((s32[]{:T(128)}, f32[4,64,2048]{2,1,0:T(8,128)}, s32[4,64]{1,0:T(4,128)S(1)}, ...), condition=%wide.region_8.9_spmd.clone, body=%wide.region_6.8_spmd.clone.sunk | while | flops 1211238400 | bytes 4611937 | solution.py:27
  79.3 4.0 exponential_reduce_fusion.2
  84.2 4.0 exponential_reduce_fusion.2
  89.2 4.0 exponential_reduce_fusion.2
  94.1 4.0 exponential_reduce_fusion.2
  100.2 19.6 %while.35 = (s32[]{:T(128)}, f32[4,16,512]{2,1,0:T(8,128)S(1)}, bf16[4,512,128]{2,1,0:T(8,128)(2,1)S(1)}, bf16[1024,128]{1,0:T(8,128)(2,1)S(1)}, f32[16,64]{1,0:T(8,128)S(1)}, /*index=5*/s32[]{:T(128)}) while((s32[]{:T(128)}, f32[4,16,512]{2,1,0:T(8,128)S(1)}, bf16[4,512,128]{2,1,0:T(8,128)(2,1)S(1)}, bf16[1024,128]{1,0:T(8,128)(2,1)S(1)}, ...), condition=%wide.region_1.2_spmd, body=%wide.region_0.1_spmd.sunk | while | flops 141041664 | bytes 8884301 | solution.py:79
  100.2 1.7 maximum_bitcast_fusion.2
  101.9 1.9 copy.41
  105.1 1.7 maximum_bitcast_fusion.2
  106.8 1.9 copy.41
  110.0 1.7 maximum_bitcast_fusion.2
  111.7 1.9 copy.41
  114.8 1.7 maximum_bitcast_fusion.2
  116.6 1.9 copy.41
  120.0 24.4 %pmax.7 = f32[16]{0:T(128)S(1)} all-reduce(f32[16]{0:T(128)S(1)} %fusion.18), channel_id=1, replica_groups=mesh['context'=16,'heads'=16] {'context'}, use_global_device_ids=true, to_apply=%region_3.4 | all-reduce | flops 16 | bytes 128 | tf_op jit(solution)/shard_map/pmax | solution.py:82
  144.5 54.5 %all-reduce.3.cloned.1.call-done = f32[256,2048]{1,0:T(8,128)} async-done(((f32[256,2048]{1,0:T(8,128)}), f32[256,2048]{1,0:T(8,128)}) %all-reduce.3.cloned.1.call-update) | async-done | bytes 2097168 | tf_op jit(solution)/shard_map/psum | solution.py:50
  200.0 24.2 %all-reduce = (f32[16]{0:T(128)S(1)}, f32[16]{0:T(128)S(1)}) all-reduce(f32[16]{0:T(128)S(1)} %dynamic-slice_reduce_fusion, f32[16]{0:T(128)S(1)} %fusion.19), channel_id=1, replica_groups=mesh['context'=16,'heads'=16] {'context'}, use_global_device_ids=true, to_apply=%region_11.12 | all-reduce | flops 32 | bytes 256 | tf_op jit(solution)/shard_map/psum | solution.py:84
  226.0 27.1 %while.37 = (s32[]{:T(128)}, f32[1024,128]{1,0:T(8,128)S(1)}, f32[4,512,128]{2,1,0:T(8,128)}, bf16[4,512,128]{2,1,0:T(8,128)(2,1)S(1)}, bf16[1024,128]{1,0:T(8,1...) while((s32[]{:T(128)}, f32[1024,128]{1,0:T(8,128)S(1)}, ...), condition=%wide.wide.region_13.14_spmd.clone, body=%wide.wide.region_12.13_spmd.clone.sunk | while | flops 405536768 | bytes 13734523 | solution.py:104
  227.0 1.9 copy.42
  228.9 2.1 select_convert_fusion.3
  233.8 1.9 copy.42
  235.6 2.1 select_convert_fusion.3
  240.5 1.9 copy.42
  242.4 2.1 select_convert_fusion.3
  247.3 1.9 copy.42
  249.2 2.1 select_convert_fusion.3
  255.0 56.0 %reduce-scatter.3.cloned.1.call-done = f32[16,4,128]{2,0,1:T(8,128)} async-done(((f32[16,64,128]{2,0,1:T(8,128)}), f32[16,4,128]{2,0,1:T(8,128)}) %reduce-scatter.3.cloned.1.call-update) | async-done | bytes 32784 | tf_op jit(solution)/shard_map/reduce_scatter | solution.py:107
  310.9 1.4 copy.28
  312.3 80.0 %reduce-scatter.5.cloned.1.call-done = f32[128,128]{1,0:T(8,128)} async-done(((f32[2048,128]{1,0:T(8,128)}), f32[128,128]{1,0:T(8,128)}) %reduce-scatter.5.cloned.1.call-update) | async-done | bytes 65552 | tf_op jit(solution)/shard_map/reduce_scatter | solution.py:108
  (75 shorter events, 26.3 us)
Async XLA Ops:
  9.9 8.9 %copy-start.4 = (s32[256]{0:T(256)S(1)}, s32[256]{0:T(256)}, u32[]{:S(2)}) copy-start(s32[256]{0:T(256)} %param.16) | copy-start | bytes 3076
  9.9 9.0 %copy-start.3 = (f32[256,8]{0,1:T(8,128)S(1)}, f32[256,8]{0,1:T(8,128)}, u32[]{:S(2)}) copy-start(f32[256,8]{0,1:T(8,128)} %param.15) | copy-start | bytes 24580
  9.9 9.2 %copy-start.2 = (f32[16,64]{1,0:T(8,128)S(1)}, f32[16,64]{1,0:T(8,128)}, u32[]{:S(2)}) copy-start(f32[16,64]{1,0:T(8,128)} %param.19) | copy-start | bytes 12292
  9.9 69.4 %copy-start.5 = (bf16[2048,576]{0,1:T(8,128)(2,1)S(1)}, bf16[2048,576]{0,1:T(8,128)(2,1)}, u32[]{:S(2)}) copy-start(bf16[2048,576]{0,1:T(8,128)(2,1)} %param.14) | copy-start | bytes 7077892
  9.9 69.4 %all-to-all-start = ((bf16[16,16,8,576]{3,2,1,0:T(8,128)(2,1)}), bf16[16,16,8,576]{3,2,1,0:T(8,128)(2,1)}, u32[]{:S(2)}, u32[]{:S(2)}) async-start(bf16[16,16,8,576]{3,2,1,0:T(8,128)(2,1)} %stack.2), calls=%async_computation | async-start | bytes 5242880 | tf_op jit(solution)/shard_map/all_to_all | solution.py:44
  18.7 180.3 %all-reduce.3.cloned.1.call-start = ((), (), s32[]{:S(2)}) async-start(), calls=%async_computation.3 | async-start | bytes 4194304 | tf_op jit(solution)/shard_map/psum | solution.py:50
  99.0 0.9 copy-start
  99.0 1.1 copy-start.1
  99.1 211.9 %reduce-scatter.3.cloned.1.call-start = ((), (), s32[]{:S(2)}) async-start(), calls=%async_computation.4 | async-start | bytes 557056 | tf_op jit(solution)/shard_map/reduce_scatter | solution.py:107
  254.2 138.0 %reduce-scatter.5.cloned.1.call-start = ((), (), s32[]{:S(2)}) async-start(), calls=%async_computation.5 | async-start | bytes 1114112 | tf_op jit(solution)/shard_map/reduce_scatter | solution.py:108
Sparse Core Ops, SparseCore 0:
  99.2 99.7 all-reduce.2
  254.3 56.5 reduce-scatter.2
  315.0 77.2 reduce-scatter.4
